TPU v7x, 32 devices: a whole 2x2x4 slice. The times are simulated.
32 devices in a mesh: row: 4 (over y, core), col: 8 (over z, x).
Axes of the slice: x: 2, y: 2, z: 4, core: 2. Of those that a mesh axis runs over, the one named last changes fastest.
Arguments:
- pair: bfloat16 [1024, 1024, 128], P('row', 'col'), may hold values from -6 to 6
- norm_gain: float32 [128], replicated, may hold values from 0.1 to 1.9
- norm_shift: float32 [128], replicated, may hold values from -3 to 3
- w_query: bfloat16 [128, 128], replicated, may hold values from -1 to 1
- w_key: bfloat16 [128, 128], replicated, may hold values from -0.5 to 0.5
- w_value: bfloat16 [128, 128], replicated, may hold values from -0.5 to 0.5
- w_gate: bfloat16 [128, 128], replicated, may hold values from -0.5 to 0.5
- gate_shift: float32 [128], replicated, may hold values from -1 to 1
- w_bias: float32 [128, 4], replicated, may hold values from -30 to 30
- w_out: bfloat16 [128, 128], replicated, may hold values from -1 to 1
- out_shift: float32 [128], replicated, may hold values from -3 to 3
Outputs:
- update: bfloat16 [1024, 1024, 128], P('row', 'col')
All inputs are finite; a program needn't handle non-finite values.
Results may differ from a plain program's by a relative error of at most 0.0015.
The roundings to bfloat16 on the way count: a program that leaves them out, or rounds other values in their place, can miss the bound.
Values may be sent and summed in bfloat16 or wider, within the bound.
A program may use at most 128 MiB of HBM per device.

v0:
```python
import functools
import math

import jax
import jax.numpy as jnp
from jax import lax
from jax.experimental import pallas as pl
from jax.experimental.pallas import tpu as pltpu
from jax.sharding import PartitionSpec as P

F32 = jnp.float32
BF16 = jnp.bfloat16
VMEM_LIMIT = 62 * 1024 * 1024


def nt_dot(a, b):
    return lax.dot_general(a, b, (((1,), (1,)), ((), ())), preferred_element_type=F32)


def norm_body(pair_ref, gain_ref, shift_ref, wbt_ref, normed_ref, bias_ref):
    rows, cols, channels = pair_ref.shape
    heads = bias_ref.shape[0]
    values = pair_ref[...].reshape(rows * cols, channels).astype(F32)
    mean = jnp.mean(values, axis=-1, keepdims=True)
    centred = values - mean
    spread = jnp.mean(centred * centred, axis=-1, keepdims=True)
    normed = (centred * lax.rsqrt(spread + 1e-05) * gain_ref[...] + shift_ref[...]).astype(BF16)
    normed_ref[...] = normed.reshape(rows, cols, channels)
    wbt = wbt_ref[...]
    high = wbt.astype(BF16)
    rest = wbt - high.astype(F32)
    mid = rest.astype(BF16)
    low = (rest - mid.astype(F32)).astype(BF16)
    bias = nt_dot(high, normed) + (nt_dot(mid, normed) + nt_dot(low, normed))
    for j in range(rows):
        bias_ref[:, j, :] = bias[:heads, j * cols : (j + 1) * cols]


def normalize(pair, gain, shift, w_bias):
    tile_rows, tile_cols, channels = pair.shape
    heads = w_bias.shape[1]
    pad = -heads % 16
    wbt = jnp.pad(w_bias.T, ((0, pad), (0, 0)))
    step = 16
    return pl.pallas_call(
        norm_body,
        grid=(tile_rows // step,),
        in_specs=[
            pl.BlockSpec((step, tile_cols, channels), lambda i: (i, 0, 0)),
            pl.BlockSpec((1, channels), lambda i: (0, 0)),
            pl.BlockSpec((1, channels), lambda i: (0, 0)),
            pl.BlockSpec(wbt.shape, lambda i: (0, 0)),
        ],
        out_specs=[
            pl.BlockSpec((step, tile_cols, channels), lambda i: (i, 0, 0)),
            pl.BlockSpec((heads, step, tile_cols), lambda i: (0, i, 0)),
        ],
        out_shape=[
            jax.ShapeDtypeStruct(pair.shape, BF16),
            jax.ShapeDtypeStruct((heads, tile_rows, tile_cols), F32),
        ],
        name="norm_bias",
    )(pair, gain[None], shift[None], wbt)


def project(x, wq_ref, wkt_ref, wv_ref, q_ref, kt_ref, v_ref, heads):
    inner = wq_ref.shape[1]
    depth = inner // heads
    query = (jnp.dot(x, wq_ref[...], preferred_element_type=F32) * (1.0 / math.sqrt(depth)))
    value = jnp.dot(x, wv_ref[...], preferred_element_type=F32)
    kt_ref[...] = nt_dot(wkt_ref[...], x).astype(BF16)
    head_of = lax.broadcasted_iota(jnp.int32, query.shape, 1) // depth
    for h in range(heads):
        q_ref[h] = jnp.where(head_of == h, query, 0.0).astype(BF16)
        v_ref[h] = jnp.where(head_of == h, value, 0.0).astype(BF16)


def attend_block(x, start, size, bias_of, q_ref, kt_ref, v_ref, wg, gshift, wo, oshift, heads):
    attended = None
    for h in range(heads):
        scores = jnp.dot(
            q_ref[h, pl.ds(start, size), :], kt_ref[...], preferred_element_type=F32
        ) + bias_of(h)
        largest = jnp.max(scores, axis=1, keepdims=True)
        raised = jnp.exp(scores - largest)
        scale = 1.0 / jnp.sum(raised, axis=1, keepdims=True)
        weights = (raised * scale).astype(BF16)
        part = jnp.dot(weights, v_ref[h], preferred_element_type=F32)
        attended = part if attended is None else attended + part
    gate = jax.nn.sigmoid(jnp.dot(x, wg, preferred_element_type=F32) + gshift)
    gated = (gate * attended).astype(BF16)
    return (jnp.dot(gated, wo, preferred_element_type=F32) + oshift).astype(BF16)


def attend_body(
    x_ref, bias_ref, wq_ref, wkt_ref, wv_ref, wg_ref, gshift_ref, wo_ref, oshift_ref,
    out_ref, q_ref, kt_ref, v_ref, x_flat, o_flat, *, block,
):
    pieces, heads = bias_ref.shape[0], bias_ref.shape[1]
    length, channels = x_flat.shape
    x_flat[...] = x_ref[...].reshape(length, channels)
    project(x_flat[...], wq_ref, wkt_ref, wv_ref, q_ref, kt_ref, v_ref, heads)

    @pl.loop(0, length // block)
    def _(b):
        start = pl.multiple_of(b * block, block)

        def bias_of(h):
            parts = [bias_ref[p, h, pl.ds(start, block), :] for p in range(pieces)]
            return parts[0] if pieces == 1 else jnp.concatenate(parts, axis=1)

        o_flat[pl.ds(start, block), :] = attend_block(
            x_flat[pl.ds(start, block), :], start, block, bias_of, q_ref, kt_ref, v_ref,
            wg_ref[...], gshift_ref[...], wo_ref[...], oshift_ref[...], heads,
        )

    out_ref[...] = o_flat[...].reshape(out_ref.shape)


def attend(rows, bias, w_query, w_key, w_value, w_gate, gate_shift, w_out, out_shift, block=512):
    groups, count, cols, channels = rows.shape
    length = groups * cols
    heads = bias.shape[1]
    inner = w_query.shape[1]
    whole = lambda a: pl.BlockSpec(a.shape, lambda i: (0,) * a.ndim, pipeline_mode=pl.Buffered(1))
    args = (bias, w_query, w_key.T, w_value, w_gate, gate_shift[None], w_out, out_shift[None])
    row_spec = pl.BlockSpec((groups, 1, cols, channels), lambda i: (0, i, 0, 0))
    return pl.pallas_call(
        functools.partial(attend_body, block=block),
        grid=(count,),
        in_specs=[row_spec] + [whole(a) for a in args],
        out_specs=row_spec,
        out_shape=jax.ShapeDtypeStruct(rows.shape, BF16),
        scratch_shapes=[
            pltpu.VMEM((heads, length, inner), BF16),
            pltpu.VMEM((inner, length), BF16),
            pltpu.VMEM((heads, length, inner), BF16),
            pltpu.VMEM((length, channels), BF16),
            pltpu.VMEM((length, channels), BF16),
        ],
        compiler_params=pltpu.CompilerParams(vmem_limit_bytes=VMEM_LIMIT),
        name="attend",
    )(rows, *args)


def on_device(
    pair, norm_gain, norm_shift, w_query, w_key, w_value, w_gate, gate_shift, w_bias, w_out,
    out_shift,
):
    col_count = lax.axis_size("col")
    row_count = lax.axis_size("row")
    tile_rows, tile_cols, channels = pair.shape
    heads = w_bias.shape[1]
    normed, tile_bias = normalize(pair, norm_gain, norm_shift, w_bias)
    by_row = lax.all_gather(tile_bias, "row", axis=1, tiled=True)
    bias = lax.all_gather(by_row, "col", axis=0)
    if tile_cols % 128:
        bias = bias.transpose(1, 2, 0, 3).reshape(1, heads, tile_rows * row_count, -1)
    blocks = normed.reshape(col_count, tile_rows // col_count, tile_cols, channels)
    rows = lax.all_to_all(blocks, "col", split_axis=0, concat_axis=0, tiled=True)
    update = attend(rows, bias, w_query, w_key, w_value, w_gate, gate_shift, w_out, out_shift)
    back = lax.all_to_all(update, "col", split_axis=0, concat_axis=0, tiled=True)
    return back.reshape(tile_rows, tile_cols, channels)


def solution(mesh):
    in_specs = (P("row", "col", None),) + (P(),) * 10
    return jax.shard_map(
        on_device, mesh=mesh, in_specs=in_specs, out_specs=P("row", "col", None), check_vma=False
    )
```

profile of v0, /device:TPU:0, one launch (start us, length us, event | category | flops | bytes accessed | tf_op | source)
XLA Modules:
  0.0 976.6 jit_solution(3065229553378948895)
XLA Ops:
  6.5 0.0 all-gather.4.cloned.1.call-start
  6.5 1.3 pad.4.wbt_ref
  7.8 18.3 %norm_bias.1 = (bf16[256,128,128]{2,1,0:T(8,128)(2,1)}, f32[4,256,128]{2,1,0:T(8,128)}) custom-call(bf16[256,128,128]{2,1,0:T(8,128)(2,1)} %pair_ref.1, f32[1,128]{1,0:T(1,128)} %bitcast.14, f32[1,128]{1,0:T(1,128)} %bitcast.15, f32[16,128]{1,0:T(8,128)} %pad.4.wbt_ref), custom_call_target="tpu_custom_call" | custom-call | tf_op jit(solution)/shard_map/norm_bias/pallas_call | solution.py:45
  26.1 0.0 all-gather.4.cloned.1.call-update
  26.1 0.0 all-gather.6.cloned.1.call-start
  26.2 25.4 %all-gather.4.cloned.1.call-done = f32[4,1024,128]{2,1,0:T(8,128)} async-done(((f32[4,256,128]{2,1,0:T(8,128)}), f32[4,1024,128]{2,1,0:T(8,128)}) %all-gather.4.cloned.1.call-update) | async-done | bytes 2097168 | tf_op jit(solution)/shard_map/all_gather | solution.py:155
  51.6 0.0 all-gather.6.cloned.1.call-update
  51.6 0.0 copy-start
  51.6 5.5 all-to-all-start
  57.1 0.0 copy-done
  57.1 0.7 copy.13
  57.9 362.8 %all-to-all-done.x_ref = bf16[8,32,128,128]{3,2,1,0:T(8,128)(2,1)} async-done(((bf16[8,32,128,128]{3,2,1,0:T(8,128)(2,1)}), bf16[8,32,128,128]{3,2,1,0:T(8,128)(2,1)}, u32[]{:S(2)}, u32[]{:S(2)}) %all-to-all-start) | async-done | bytes 8388640 | tf_op jit(solution)/shard_map/all_to_all | solution.py:160
  420.7 22.9 %all-gather.6.cloned.1.call-done = f32[32,1024,128]{2,1,0:T(8,128)} async-done(((f32[4,1024,128]{2,1,0:T(8,128)}), f32[32,1024,128]{2,1,0:T(8,128)}) %all-gather.6.cloned.1.call-update) | async-done | bytes 16777232 | tf_op jit(solution)/shard_map/all_gather | solution.py:156
  443.6 326.4 %attend.1 = bf16[8,32,128,128]{3,2,1,0:T(8,128)(2,1)} custom-call(bf16[8,32,128,128]{3,2,1,0:T(8,128)(2,1)} %all-to-all-done.x_ref, f32[8,4,1024,128]{3,2,1,0:T(8,128)} %bitcast.10, bf16[128,128]{1,0:T(8,128)(2,1)} %wq_ref.1, bf16[128,128]{1,0:T(8,128)(2,1)} %bitcast.12, bf16[128,128]{1,0:T(8,128)(2,1)} %wv_ref.1, bf16[128,128]{1,0:T(8,128)(2,1)} %wg_ref.1, ...), custom_call_target="tpu_custom_call" | custom-call | tf_op jit(solution)/shard_map/attend/pallas_call | solution.py:128
  770.0 189.2 %all_to_all.10 = bf16[8,32,128,128]{3,2,1,0:T(8,128)(2,1)} all-to-all(bf16[8,32,128,128]{3,2,1,0:T(8,128)(2,1)} %attend.1), channel_id=1, replica_groups=mesh['row'=4,'col'=8] {'col'}, dimensions={0} | all-to-all | bytes 16777216 | tf_op jit(solution)/shard_map/all_to_all | solution.py:162
  959.2 10.5 %copy.15 = bf16[256,128,128]{2,1,0:T(8,128)(2,1)} copy(bf16[256,128,128]{2,1,0:T(8,128)(2,1)} %bitcast.9) | data formatting | bytes 16777216
Async XLA Ops:
  6.5 45.0 %all-gather.4.cloned.1.call-start = ((), (), s32[]{:S(2)}) async-start(), calls=%async_computation.2 | async-start | bytes 2621440 | tf_op jit(solution)/shard_map/all_gather | solution.py:155
  26.1 417.4 %all-gather.6.cloned.1.call-start = ((), (), s32[]{:S(2)}) async-start(), calls=%async_computation.3 | async-start | bytes 18874368 | tf_op jit(solution)/shard_map/all_gather | solution.py:156
  51.6 5.5 copy-start
  51.6 369.0 %all-to-all-start = ((bf16[8,32,128,128]{3,2,1,0:T(8,128)(2,1)}), bf16[8,32,128,128]{3,2,1,0:T(8,128)(2,1)}, u32[]{:S(2)}, u32[]{:S(2)}) async-start(bf16[8,32,128,128]{3,2,1,0:T(8,128)(2,1)} %bitcast.11), calls=%async_computation | async-start | bytes 16777216 | tf_op jit(solution)/shard_map/all_to_all | solution.py:160
Sparse Core Ops, SparseCore 0:
  26.3 25.2 all-gather.3
  53.7 389.8 all-gather.5
where the time goes:
time: 977 us
  waiting for transfers between devices  411 us (42%)
  Pallas kernels  345 us (35%)
  blocking collectives  189 us (19%)
  between operations  13.4 us (1%)
  local copies, waits for them, and re-layouts  12.5 us (1%)
    all_to_all x1, waiting for transfers between devices, on_device(): lax.all_to_all(blocks, 'col', split_axis=0, concat_axis=0, tiled=True)  363 us
    pallas_call x1, Pallas kernels, attend(): pl.pallas_call(functools.partial(attend_body, block=block), grid=(count,)...  326 us
    all_to_all x1, blocking collectives, on_device(): lax.all_to_all(update, 'col', split_axis=0, concat_axis=0, tiled=True)  189 us
    all_gather x1, waiting for transfers between devices, on_device(): by_row = lax.all_gather(tile_bias, 'row', axis=1, tiled=True)  25.4 us
    all_gather x1, waiting for transfers between devices, on_device(): bias = lax.all_gather(by_row, 'col', axis=0)  22.9 us
  transfers between devices with their start and end apart: 3, of which 3 were waited for; matrix products, arithmetic and copies ran while one was open for 0% of the time, Pallas kernels for 0%

commit v1 on v0

v1 whole, which is shorter than its diff:
```python
import functools
import math

import jax
import jax.numpy as jnp
from jax import lax
from jax.experimental import pallas as pl
from jax.experimental.pallas import tpu as pltpu
from jax.sharding import PartitionSpec as P

F32 = jnp.float32
BF16 = jnp.bfloat16
VMEM_LIMIT = 62 * 1024 * 1024
LOG2E = math.log2(math.e)
MESH = pl.DeviceIdType.MESH


def nt_dot(a, b):
    return lax.dot_general(a, b, (((1,), (1,)), ((), ())), preferred_element_type=F32)


def layer_norm(values, gain, shift):
    mean = jnp.mean(values, axis=-1, keepdims=True)
    centred = values - mean
    spread = jnp.mean(centred * centred, axis=-1, keepdims=True)
    return (centred * lax.rsqrt(spread + 1e-05) * gain + shift).astype(BF16)


def split_bias_weights(wbt):
    high = wbt.astype(BF16)
    rest = wbt - high.astype(F32)
    mid = rest.astype(BF16)
    low = (rest - mid.astype(F32)).astype(BF16)
    return high, mid, low


def project(x, wq_ref, wkt_ref, wv_ref, q_ref, kt_ref, v_ref, heads):
    length, inner = x.shape[0], wq_ref.shape[1]
    depth = inner // heads
    query = jnp.dot(x, wq_ref[...], preferred_element_type=F32) * (1.0 / math.sqrt(depth))
    query = query.astype(BF16).astype(F32) * LOG2E
    high = query.astype(BF16)
    low = (query - high.astype(F32)).astype(BF16)
    value = jnp.dot(x, wv_ref[...], preferred_element_type=F32).astype(BF16)
    key_t = nt_dot(wkt_ref[...], x).astype(BF16)
    kt_ref[:inner] = key_t
    kt_ref[inner:] = key_t
    head_of = lax.broadcasted_iota(jnp.int32, query.shape, 1) // depth
    zero = jnp.zeros_like(high)
    for h in range(heads):
        q_ref[h, :, :inner] = jnp.where(head_of == h, high, zero)
        q_ref[h, :, inner:] = jnp.where(head_of == h, low, zero)
        v_ref[h * length : (h + 1) * length] = jnp.where(head_of == h, value, zero)


def attend_block(x, start, block, bias_ref, q_ref, kt_ref, v_ref, s_ref, w_ref, wg, gshift, group):
    pieces, heads, _, cols = bias_ref.shape
    length = kt_ref.shape[1]
    wide = max(128, cols)
    tile = max(length // 4, wide)
    for h in range(heads):
        for t in range(length // tile):
            scores = jnp.dot(
                q_ref[h, pl.ds(start, block), :],
                kt_ref[:, t * tile : (t + 1) * tile],
                preferred_element_type=F32,
            )
            for u in range(tile // wide):
                at = t * tile + u * wide
                parts = [
                    bias_ref[p, h, pl.ds(start, block), :]
                    for p in range(at // cols, (at + wide) // cols)
                ]
                bias = parts[0] if len(parts) == 1 else jnp.concatenate(parts, axis=1)
                s_ref[h, :, at : at + wide] = scores[:, u * wide : (u + 1) * wide] + bias

        def normalize_group(g, carry):
            at = pl.multiple_of(g * group, group)
            scores = s_ref[h, pl.ds(at, group), :]
            largest = jnp.max(scores, axis=1, keepdims=True)
            raised = jnp.exp2(scores - largest)
            scale = 1.0 / jnp.sum(raised, axis=1, keepdims=True)
            w_ref[pl.ds(at, group), h * length : (h + 1) * length] = (raised * scale).astype(BF16)
            return carry

        lax.fori_loop(0, block // group, normalize_group, 0, unroll=True)
    attended = jnp.dot(w_ref[...], v_ref[...], preferred_element_type=F32)
    gate = jax.nn.sigmoid(jnp.dot(x, wg, preferred_element_type=F32) + gshift)
    return (gate * attended).astype(BF16)


def fused_body(
    pair_ref, gain_ref, shift_ref, wbt_ref, wq_ref, wkt_ref, wv_ref, wg_ref, gshift_ref,
    gated_ref,
    xs_ref, xr_ref, bias_ref, q_ref, kt_ref, v_ref, s_ref, w_ref, g_ref,
    load_sem, x_send, x_recv, own_sem, b_recv, up_send, down_send, side_send, y_send, core_send,
    g_send, g_recv, g_own, *, chunk, block,
):
    n, rows, cols, channels = xs_ref.shape
    heads = bias_ref.shape[1]
    length = n * cols
    tile_rows = n * rows
    r, c = lax.axis_index("row"), lax.axis_index("col")
    row_count = lax.axis_size("row")
    lows = 2 if n % 2 == 0 else 1
    highs = n // lows
    cores = 2 if row_count % 2 == 0 else 1
    planes = row_count // cores
    z, low = c // lows, c % lows
    y, core = r // cores, r % cores
    chunks = rows // chunk

    def load(k):
        part = pl.ds(k * chunk, chunk)
        return pltpu.make_async_copy(pair_ref.at[:, part], xs_ref.at[:, part], load_sem.at[k])

    for k in range(chunks):
        load(k).start()

    high_w, mid_w, low_w = split_bias_weights(wbt_ref[...])

    def norm_chunk(k):
        load(k).wait()

        @pl.loop(0, n)
        def _(t):
            part = pl.ds(k * chunk, chunk)
            values = xs_ref[t, part].reshape(chunk * cols, channels).astype(F32)
            normed = layer_norm(values, gain_ref[...], shift_ref[...])
            xs_ref[t, part] = normed.reshape(chunk, cols, channels)
            bias = nt_dot(high_w, normed) + (nt_dot(mid_w, normed) + nt_dot(low_w, normed))
            bias = bias * LOG2E
            base = r * tile_rows + t * rows + k * chunk
            for j in range(chunk):
                bias_ref[c, :, base + j, :] = bias[:heads, j * cols : (j + 1) * cols]

    def x_copy(k, p):
        to = lax.rem(c + p, n)
        part = pl.ds(k * chunk, chunk)
        return pltpu.make_async_remote_copy(
            src_ref=xs_ref.at[to, part], dst_ref=xr_ref.at[part, c],
            send_sem=x_send.at[p, k], recv_sem=x_recv.at[p, k],
            device_id=(r, to), device_id_type=MESH,
        )

    def x_own(k):
        part = pl.ds(k * chunk, chunk)
        return pltpu.make_async_copy(xs_ref.at[c, part], xr_ref.at[part, c], own_sem.at[k])

    def send_x(k):
        for p in range(1, n):
            x_copy(k, p).start()
        x_own(k).start()

    def piece(row, col):
        return bias_ref.at[col, :, pl.ds(row * tile_rows, tile_rows), :]

    def b_copy(row, col, to, sem):
        return pltpu.make_async_remote_copy(
            src_ref=piece(row, col), dst_ref=piece(row, col), send_sem=sem,
            recv_sem=b_recv.at[row, col], device_id=to, device_id_type=MESH,
        )

    def b_wait(row, col):
        b_copy(row, col, (r, c), core_send.at[0, 0]).wait_recv()

    def up_copy(a):
        return b_copy(r, a * lows + low, (r, c + lows), up_send.at[a])

    def down_copy(a):
        return b_copy(r, a * lows + low, (r, c - lows), down_send.at[a])

    def side_copy(a):
        return b_copy(r, a * lows + low, (r, z * lows + 1 - low), side_send.at[a])

    def y_copy(q, col):
        return b_copy(r, col, (lax.rem(y + q, planes) * cores + core, c), y_send.at[q, col])

    def core_copy(plane, col):
        return b_copy(
            plane * cores + core, col, (y * cores + 1 - core, c), core_send.at[plane, col]
        )

    def forward_rows(col):
        for q in range(1, planes):
            y_copy(q, col).start()
        if cores == 2:
            core_copy(y, col).start()

    def forward_line(a):
        if lows == 2:
            side_copy(a).start()
        forward_rows(a * lows + low)

    norm_chunk(0)
    send_x(0)
    for k in range(1, chunks):
        norm_chunk(k)

    @pl.when(z < highs - 1)
    def _():
        up_copy(z).start()

    @pl.when(z > 0)
    def _():
        down_copy(z).start()

    forward_line(z)
    if chunks > 1:
        send_x(1)
    for k in range(1, highs):

        @pl.when(z - k >= 0)
        def _():
            b_wait(r, (z - k) * lows + low)

            @pl.when(z < highs - 1)
            def _():
                up_copy(z - k).start()

            forward_line(z - k)

        @pl.when(z + k < highs)
        def _():
            b_wait(r, (z + k) * lows + low)

            @pl.when(z > 0)
            def _():
                down_copy(z + k).start()

            forward_line(z + k)

    for k in range(2, chunks):
        send_x(k)
    if lows == 2:

        @pl.loop(0, highs)
        def _(a):
            col = a * lows + 1 - low
            b_wait(r, col)
            forward_rows(col)

    for q in range(1, planes):

        @pl.loop(0, n)
        def _(col):
            plane = lax.rem(y + planes - q, planes)
            b_wait(plane * cores + core, col)
            if cores == 2:
                core_copy(plane, col).start()

    if cores == 2:

        @pl.loop(0, planes * n)
        def _(i):
            b_wait((i // n) * cores + 1 - core, i % n)

    def g_copy(s, p):
        to = lax.rem(c + p, n)
        return pltpu.make_async_remote_copy(
            src_ref=g_ref.at[s, to], dst_ref=gated_ref.at[c, s],
            send_sem=g_send.at[p], recv_sem=g_recv.at[p],
            device_id=(r, to), device_id_type=MESH,
        )

    def attend_row(s):
        x = xr_ref[s].reshape(length, channels)
        project(x, wq_ref, wkt_ref, wv_ref, q_ref, kt_ref, v_ref, heads)
        groups = block // cols
        for b in range(length // block):
            part = pl.ds(b * groups, groups)
            gated = attend_block(
                xr_ref[s, part].reshape(block, channels), b * block, block, bias_ref, q_ref,
                kt_ref, v_ref, s_ref, w_ref, wg_ref[...], gshift_ref[...], 16,
            )
            g_ref[s, part] = gated.reshape(groups, cols, channels)

    @pl.loop(0, chunks)
    def _(k):
        for p in range(1, n):
            x_copy(k, p).wait_recv()
        x_own(k).wait()

        @pl.loop(0, chunk)
        def _(i):
            s = k * chunk + i
            attend_row(s)
            for p in range(1, n):
                g_copy(s, p).start()
            pltpu.make_async_copy(g_ref.at[s, c], gated_ref.at[c, s], g_own).start()

    for p in range(1, n):
        to, origin = lax.rem(c + p, n), lax.rem(c + n - p, n)
        pltpu.make_async_remote_copy(
            src_ref=g_ref.at[:, to], dst_ref=gated_ref.at[origin],
            send_sem=g_send.at[p], recv_sem=g_recv.at[p],
            device_id=(r, to), device_id_type=MESH,
        ).wait()
    pltpu.make_async_copy(g_ref.at[:, c], gated_ref.at[c], g_own).wait()

    @pl.loop(0, chunks)
    def _(k):
        for p in range(1, n):
            x_copy(k, p).wait_send()

    @pl.loop(0, highs)
    def _(a):
        if lows == 2:
            side_copy(a).wait_send()

        @pl.when((z < highs - 1) & (a <= z))
        def _():
            up_copy(a).wait_send()

        @pl.when((z > 0) & (a >= z))
        def _():
            down_copy(a).wait_send()

    @pl.loop(0, n)
    def _(col):
        for q in range(1, planes):
            y_copy(q, col).wait_send()
        if cores == 2:
            for plane in range(planes):
                core_copy(plane, col).wait_send()


def gated_attention(
    pair, norm_gain, norm_shift, w_query, w_key, w_value, w_gate, gate_shift, w_bias,
):
    n, row_count = lax.axis_size("col"), lax.axis_size("row")
    tile_rows, cols, channels = pair.shape
    rows = tile_rows // n
    length = n * cols
    heads, inner = w_bias.shape[1], w_query.shape[1]
    chunk = math.gcd(rows, 8)
    block = math.gcd(length, 512)
    wbt = jnp.pad(w_bias.T, ((0, -heads % 16), (0, 0)))
    tiled = (n, rows, cols, channels)
    highs, planes = n // (2 if n % 2 == 0 else 1), row_count // (2 if row_count % 2 == 0 else 1)
    dma = pltpu.SemaphoreType.DMA
    vmem = pl.BlockSpec(memory_space=pltpu.VMEM)
    anywhere = pl.BlockSpec(memory_space=pl.ANY)
    return pl.pallas_call(
        functools.partial(fused_body, chunk=chunk, block=block),
        in_specs=[anywhere] + [vmem] * 8,
        out_specs=anywhere,
        out_shape=jax.ShapeDtypeStruct(tiled, BF16),
        scratch_shapes=[
            pltpu.VMEM(tiled, BF16),
            pltpu.VMEM((rows, n, cols, channels), BF16),
            pltpu.VMEM((n, heads, tile_rows * row_count, cols), F32),
            pltpu.VMEM((heads, length, 2 * inner), BF16),
            pltpu.VMEM((2 * inner, length), BF16),
            pltpu.VMEM((heads * length, inner), BF16),
            pltpu.VMEM((heads, block, length), F32),
            pltpu.VMEM((block, heads * length), BF16),
            pltpu.VMEM((rows, n, cols, channels), BF16),
            dma((rows // chunk,)),
            dma((n, rows // chunk)),
            dma((n, rows // chunk)),
            dma((rows // chunk,)),
            dma((row_count, n)),
            dma((highs,)),
            dma((highs,)),
            dma((highs,)),
            dma((planes, n)),
            dma((planes, n)),
            dma((n,)),
            dma((n,)),
            dma(()),
        ],
        compiler_params=pltpu.CompilerParams(
            has_side_effects=True, vmem_limit_bytes=VMEM_LIMIT
        ),
        name="gated_attention",
    )(
        pair.reshape(tiled), norm_gain[None], norm_shift[None], wbt, w_query, w_key.T, w_value,
        w_gate, gate_shift[None],
    )


def out_body(gated_ref, wo_ref, oshift_ref, out_ref):
    rows, cols, channels = out_ref.shape
    gated = gated_ref[...].reshape(rows * cols, -1)
    update = jnp.dot(gated, wo_ref[...], preferred_element_type=F32) + oshift_ref[...]
    out_ref[...] = update.astype(BF16).reshape(rows, cols, channels)


def project_out(gated, w_out, out_shift):
    tile_rows, cols, inner = gated.shape
    channels = w_out.shape[1]
    step = math.gcd(tile_rows, 32)
    return pl.pallas_call(
        out_body,
        grid=(tile_rows // step,),
        in_specs=[
            pl.BlockSpec((step, cols, inner), lambda i: (i, 0, 0)),
            pl.BlockSpec((inner, channels), lambda i: (0, 0)),
            pl.BlockSpec((1, channels), lambda i: (0, 0)),
        ],
        out_specs=pl.BlockSpec((step, cols, channels), lambda i: (i, 0, 0)),
        out_shape=jax.ShapeDtypeStruct((tile_rows, cols, channels), BF16),
        name="project_out",
    )(gated, w_out, out_shift[None])


def on_device(
    pair, norm_gain, norm_shift, w_query, w_key, w_value, w_gate, gate_shift, w_bias, w_out,
    out_shift,
):
    gated = gated_attention(
        pair, norm_gain, norm_shift, w_query, w_key, w_value, w_gate, gate_shift, w_bias
    )
    return project_out(gated.reshape(pair.shape[:2] + (-1,)), w_out, out_shift)


def solution(mesh):
    in_specs = (P("row", "col", None),) + (P(),) * 10
    return jax.shard_map(
        on_device, mesh=mesh, in_specs=in_specs, out_specs=P("row", "col", None), check_vma=False
    )
```

time: 977 us -> 479 us (0.49)
  waiting for transfers between devices: 411 us -> 0 us
  blocking collectives: 189 us -> 0 us
  Pallas kernels: 345 us -> 475 us
  between operations: 13.4 us -> 0.01 us
    all_to_all x1 -> x0, waiting for transfers between devices: 363 us -> none  [on_device(): lax.all_to_all(blocks, 'col', split_axis=0, concat_axis=0, tiled=True)]
    all_to_all x1 -> x0, blocking collectives: 189 us -> none  [on_device(): lax.all_to_all(update, 'col', split_axis=0, concat_axis=0, tiled=True)]
    pallas_call x2, Pallas kernels: 345 us -> 475 us  [the longest x1 464 us: gated_attention(): pl.pallas_call(functools.partial(fused_body, chunk=chunk, block=block), i...]
    all_gather x2 -> x0, waiting for transfers between devices: 48.3 us -> none  [the longest x1 25.4 us: on_device(): by_row = lax.all_gather(tile_bias, 'row', axis=1, tiled=True)]
  transfers between devices with their start and end apart: 3 -> 0, of which waited for: 3 -> 0; matrix products, arithmetic and copies ran while one was open for 0% -> 0% of each run, Pallas kernels for 0% -> 0%
where the time goes in v1:
time: 479 us; the launch traced here: 478 us
  Pallas kernels  475 us (99%)
    pallas_call x1, Pallas kernels, gated_attention(): pl.pallas_call(functools.partial(fused_body, chunk=chunk, block=block), i...  464 us
    pallas_call x1, Pallas kernels, project_out(): pl.pallas_call(out_body, grid=(tile_rows // step,), in_specs=[pl.BlockSpe...  10.3 us

profile of v1, /device:TPU:0, one launch (start us, length us, event | category | flops | bytes accessed | tf_op | source)
XLA Modules:
  0.0 477.6 jit_solution(2118293369054559006)
XLA Ops:
  0.0 1.3 pad.4.wbt_ref
  1.3 1.5 copy.12
  2.8 464.5 %gated_attention.1 = bf16[8,32,128,128]{3,2,1,0:T(8,128)(2,1)} custom-call(bf16[8,32,128,128]{3,2,1,0:T(8,128)(2,1)} %bitcast.9, f32[1,128]{1,0:T(1,128)} %bitcast.12, f32[1,128]{1,0:T(1,128)} %bitcast.13, f32[16,128]{1,0:T(8,128)} %pad.4.wbt_ref, bf16[128,128]{1,0:T(8,128)(2,1)} %wq_ref.1, bf16[128,128]{1,0:T(8,128)(2,1)} %bitcast.10, ...), custom_call_target="tpu_custom_call" | custom-call | tf_op jit(solution)/shard_map/gated_attention/pallas_call | solution.py:344
  467.2 10.3 %project_out.1 = bf16[256,128,128]{2,1,0:T(8,128)(2,1)} custom-call(bf16[256,128,128]{2,1,0:T(8,128)(2,1)} %bitcast.8, bf16[128,128]{1,0:T(8,128)(2,1)} %wo_ref.1, f32[1,128]{1,0:T(1,128)} %bitcast.15), custom_call_target="tpu_custom_call" | custom-call | tf_op jit(solution)/shard_map/project_out/pallas_call | solution.py:394

commit v2 on v1

--- a/solution.py
+++ b/solution.py
@@ -34,67 +34,91 @@
     return high, mid, low
 
 
-def project(x, wq_ref, wkt_ref, wv_ref, q_ref, kt_ref, v_ref, heads):
-    length, inner = x.shape[0], wq_ref.shape[1]
+def project(x_ref, starts, block, wqv_ref, wkt_ref, q_ref, kt_ref, v_ref):
+    heads, length, inner = v_ref.shape
+    groups, cols, channels = x_ref.shape
     depth = inner // heads
-    query = jnp.dot(x, wq_ref[...], preferred_element_type=F32) * (1.0 / math.sqrt(depth))
-    query = query.astype(BF16).astype(F32) * LOG2E
-    high = query.astype(BF16)
-    low = (query - high.astype(F32)).astype(BF16)
-    value = jnp.dot(x, wv_ref[...], preferred_element_type=F32).astype(BF16)
+    x = x_ref[...].reshape(length, channels)
     key_t = nt_dot(wkt_ref[...], x).astype(BF16)
     kt_ref[:inner] = key_t
     kt_ref[inner:] = key_t
-    head_of = lax.broadcasted_iota(jnp.int32, query.shape, 1) // depth
-    zero = jnp.zeros_like(high)
+    if len(starts) * block == length:
+        both = jnp.dot(x, wqv_ref[...], preferred_element_type=F32)
+        value = both[:, inner:]
+        queries = [(pl.ds(0, length), both[:, :inner])]
+    else:
+        value = jnp.dot(x, wqv_ref[:, inner:], preferred_element_type=F32)
+        queries = []
+        for start in starts:
+            part = x_ref[pl.ds(start // cols, block // cols)].reshape(block, channels)
+            query = jnp.dot(part, wqv_ref[:, :inner], preferred_element_type=F32)
+            queries.append((pl.ds(start, block), query))
+    value = value.astype(BF16)
+    head_of = lax.broadcasted_iota(jnp.int32, value.shape, 1) // depth
     for h in range(heads):
-        q_ref[h, :, :inner] = jnp.where(head_of == h, high, zero)
-        q_ref[h, :, inner:] = jnp.where(head_of == h, low, zero)
-        v_ref[h * length : (h + 1) * length] = jnp.where(head_of == h, value, zero)
-
-
-def attend_block(x, start, block, bias_ref, q_ref, kt_ref, v_ref, s_ref, w_ref, wg, gshift, group):
+        v_ref[h] = jnp.where(head_of == h, value, jnp.zeros_like(value))
+    for part, query in queries:
+        query = query * (1.0 / math.sqrt(depth))
+        query = query.astype(BF16).astype(F32) * LOG2E
+        high = query.astype(BF16)
+        low = (query - high.astype(F32)).astype(BF16)
+        head_of = lax.broadcasted_iota(jnp.int32, high.shape, 1) // depth
+        zero = jnp.zeros_like(high)
+        for h in range(heads):
+            q_ref[h, part, :inner] = jnp.where(head_of == h, high, zero)
+            q_ref[h, part, inner:] = jnp.where(head_of == h, low, zero)
+
+
+def attend(starts, block, bias_ref, q_ref, kt_ref, v_ref, s_ref, w_ref, sum_ref, group=16):
     pieces, heads, _, cols = bias_ref.shape
     length = kt_ref.shape[1]
     wide = max(128, cols)
-    tile = max(length // 4, wide)
-    for h in range(heads):
-        for t in range(length // tile):
-            scores = jnp.dot(
-                q_ref[h, pl.ds(start, block), :],
-                kt_ref[:, t * tile : (t + 1) * tile],
-                preferred_element_type=F32,
-            )
-            for u in range(tile // wide):
-                at = t * tile + u * wide
-                parts = [
-                    bias_ref[p, h, pl.ds(start, block), :]
-                    for p in range(at // cols, (at + wide) // cols)
-                ]
-                bias = parts[0] if len(parts) == 1 else jnp.concatenate(parts, axis=1)
-                s_ref[h, :, at : at + wide] = scores[:, u * wide : (u + 1) * wide] + bias
-
-        def normalize_group(g, carry):
-            at = pl.multiple_of(g * group, group)
-            scores = s_ref[h, pl.ds(at, group), :]
+    items = [(b, h) for b in range(len(starts)) for h in range(heads)]
+
+    def scores_of(i):
+        b, h = items[i]
+        part = pl.ds(starts[b], block)
+        scores = jnp.dot(q_ref[h, part, :], kt_ref[...], preferred_element_type=F32)
+        for at in range(0, length, wide):
+            parts = [bias_ref[p, h, part, :] for p in range(at // cols, (at + wide) // cols)]
+            bias = parts[0] if len(parts) == 1 else jnp.concatenate(parts, axis=1)
+            s_ref[i % 2, :, at : at + wide] = scores[:, at : at + wide] + bias
+
+    def softmax_of(i):
+        def one_group(g, carry):
+            part = pl.ds(pl.multiple_of(g * group, group), group)
+            scores = s_ref[i % 2, part, :]
             largest = jnp.max(scores, axis=1, keepdims=True)
             raised = jnp.exp2(scores - largest)
             scale = 1.0 / jnp.sum(raised, axis=1, keepdims=True)
-            w_ref[pl.ds(at, group), h * length : (h + 1) * length] = (raised * scale).astype(BF16)
+            w_ref[i % 2, part, :] = (raised * scale).astype(BF16)
             return carry
 
-        lax.fori_loop(0, block // group, normalize_group, 0, unroll=True)
-    attended = jnp.dot(w_ref[...], v_ref[...], preferred_element_type=F32)
-    gate = jax.nn.sigmoid(jnp.dot(x, wg, preferred_element_type=F32) + gshift)
-    return (gate * attended).astype(BF16)
+        lax.fori_loop(0, block // group, one_group, 0, unroll=True)
+
+    def values_of(i):
+        b, h = items[i]
+        part = jnp.dot(w_ref[i % 2], v_ref[h], preferred_element_type=F32)
+        if h == 0:
+            sum_ref[b] = part
+        else:
+            sum_ref[b] += part
+
+    for step in range(len(items) + 2):
+        if step >= 2:
+            values_of(step - 2)
+        if step < len(items):
+            scores_of(step)
+        if 1 <= step <= len(items):
+            softmax_of(step - 1)
 
 
 def fused_body(
-    pair_ref, gain_ref, shift_ref, wbt_ref, wq_ref, wkt_ref, wv_ref, wg_ref, gshift_ref,
+    pair_ref, gain_ref, shift_ref, wbt_ref, wqv_ref, wkt_ref, wg_ref, gshift_ref,
     gated_ref,
-    xs_ref, xr_ref, bias_ref, q_ref, kt_ref, v_ref, s_ref, w_ref, g_ref,
+    xs_ref, xr_ref, bias_ref, q_ref, kt_ref, v_ref, s_ref, w_ref, sum_ref, g_ref,
     load_sem, x_send, x_recv, own_sem, b_recv, up_send, down_send, side_send, y_send, core_send,
-    g_send, g_recv, g_own, *, chunk, block,
+    g_send, g_recv, g_own, *, chunk,
 ):
     n, rows, cols, channels = xs_ref.shape
     heads = bias_ref.shape[1]
@@ -109,6 +133,7 @@
     z, low = c // lows, c % lows
     y, core = r // cores, r % cores
     chunks = rows // chunk
+    block = length // planes
 
     def load(k):
         part = pl.ds(k * chunk, chunk)
@@ -192,6 +217,13 @@
             side_copy(a).start()
         forward_rows(a * lows + low)
 
+    waiting = list(range(1, chunks))
+
+    def send_some(count):
+        for k in waiting[:count]:
+            send_x(k)
+        del waiting[:count]
+
     norm_chunk(0)
     send_x(0)
     for k in range(1, chunks):
@@ -206,8 +238,7 @@
         down_copy(z).start()
 
     forward_line(z)
-    if chunks > 1:
-        send_x(1)
+    send_some(1)
     for k in range(1, highs):
 
         @pl.when(z - k >= 0)
@@ -230,8 +261,7 @@
 
             forward_line(z + k)
 
-    for k in range(2, chunks):
-        send_x(k)
+    send_some(2)
     if lows == 2:
 
         @pl.loop(0, highs)
@@ -240,20 +270,30 @@
             b_wait(r, col)
             forward_rows(col)
 
-    for q in range(1, planes):
+    send_some(2)
+    if cores == 2:
 
         @pl.loop(0, n)
         def _(col):
-            plane = lax.rem(y + planes - q, planes)
-            b_wait(plane * cores + core, col)
-            if cores == 2:
-                core_copy(plane, col).start()
-
-    if cores == 2:
-
-        @pl.loop(0, planes * n)
-        def _(i):
-            b_wait((i // n) * cores + 1 - core, i % n)
+            b_wait(y * cores + 1 - core, col)
+
+    def forward_planes():
+        for q in range(1, planes):
+
+            @pl.loop(0, n)
+            def _(col):
+                plane = lax.rem(y + planes - q, planes)
+                b_wait(plane * cores + core, col)
+                if cores == 2:
+                    core_copy(plane, col).start()
+
+    def await_planes():
+        if cores == 2:
+            for q in range(1, planes):
+
+                @pl.loop(0, n)
+                def _(col):
+                    b_wait(lax.rem(y + q, planes) * cores + 1 - core, col)
 
     def g_copy(s, p):
         to = lax.rem(c + p, n)
@@ -263,31 +303,68 @@
             device_id=(r, to), device_id_type=MESH,
         )
 
-    def attend_row(s):
-        x = xr_ref[s].reshape(length, channels)
-        project(x, wq_ref, wkt_ref, wv_ref, q_ref, kt_ref, v_ref, heads)
+    def attend_row(s, nth):
+        starts = [pl.multiple_of(lax.rem(y + q, planes) * block, block) for q in nth]
+        project(xr_ref.at[s], starts, block, wqv_ref, wkt_ref, q_ref, kt_ref, v_ref)
+        attend(starts, block, bias_ref, q_ref, kt_ref, v_ref, s_ref, w_ref, sum_ref)
         groups = block // cols
-        for b in range(length // block):
-            part = pl.ds(b * groups, groups)
-            gated = attend_block(
-                xr_ref[s, part].reshape(block, channels), b * block, block, bias_ref, q_ref,
-                kt_ref, v_ref, s_ref, w_ref, wg_ref[...], gshift_ref[...], 16,
-            )
-            g_ref[s, part] = gated.reshape(groups, cols, channels)
-
-    @pl.loop(0, chunks)
-    def _(k):
+        for b, start in enumerate(starts):
+            first = start // cols
+            x = xr_ref[s, pl.ds(first, groups)].reshape(block, channels)
+            gate = jnp.dot(x, wg_ref[...], preferred_element_type=F32) + gshift_ref[...]
+            gated = (jax.nn.sigmoid(gate) * sum_ref[b]).astype(BF16)
+            g_ref[s, pl.ds(first, groups)] = gated.reshape(groups, cols, channels)
+
+    def send_row(s, nth):
+        groups = block // cols
+        for q in nth:
+
+            @pl.loop(0, groups)
+            def _(i):
+                p = lax.rem(lax.rem(y + q, planes) * groups + i + n - c, n)
+
+                @pl.when(p > 0)
+                def _():
+                    g_copy(s, p).start()
+
+                @pl.when(p == 0)
+                def _():
+                    pltpu.make_async_copy(g_ref.at[s, c], gated_ref.at[c, s], g_own).start()
+
+    def attend_chunks(first, last, nth):
+        @pl.loop(first * chunk, last * chunk)
+        def _(s):
+            attend_row(s, nth)
+            send_row(s, nth)
+
+    def await_rows(k):
         for p in range(1, n):
             x_copy(k, p).wait_recv()
         x_own(k).wait()
 
-        @pl.loop(0, chunk)
-        def _(i):
-            s = k * chunk + i
-            attend_row(s)
-            for p in range(1, n):
-                g_copy(s, p).start()
-            pltpu.make_async_copy(g_ref.at[s, c], gated_ref.at[c, s], g_own).start()
+    early = max(1, chunks // 2)
+    mine, others = (0,), tuple(range(1, planes))
+    first = max(1, early // 2)
+
+    def attend_own(start, stop):
+        @pl.loop(start, stop)
+        def _(k):
+            await_rows(k)
+            attend_chunks(k, k + 1, mine)
+
+    attend_own(0, first)
+    send_some(chunks)
+    forward_planes()
+    if first < early:
+        attend_own(first, early)
+    await_planes()
+    if others:
+        attend_chunks(0, early, others)
+
+    @pl.loop(early, chunks)
+    def _(k):
+        await_rows(k)
+        attend_chunks(k, k + 1, mine + others)
 
     for p in range(1, n):
         to, origin = lax.rem(c + p, n), lax.rem(c + n - p, n)
@@ -333,17 +410,18 @@
     rows = tile_rows // n
     length = n * cols
     heads, inner = w_bias.shape[1], w_query.shape[1]
-    chunk = math.gcd(rows, 8)
-    block = math.gcd(length, 512)
+    chunk = math.gcd(rows, 4)
     wbt = jnp.pad(w_bias.T, ((0, -heads % 16), (0, 0)))
     tiled = (n, rows, cols, channels)
-    highs, planes = n // (2 if n % 2 == 0 else 1), row_count // (2 if row_count % 2 == 0 else 1)
+    planes = row_count // (2 if row_count % 2 == 0 else 1)
+    block = length // planes
+    highs = n // (2 if n % 2 == 0 else 1)
     dma = pltpu.SemaphoreType.DMA
     vmem = pl.BlockSpec(memory_space=pltpu.VMEM)
     anywhere = pl.BlockSpec(memory_space=pl.ANY)
     return pl.pallas_call(
-        functools.partial(fused_body, chunk=chunk, block=block),
-        in_specs=[anywhere] + [vmem] * 8,
+        functools.partial(fused_body, chunk=chunk),
+        in_specs=[anywhere] + [vmem] * 7,
         out_specs=anywhere,
         out_shape=jax.ShapeDtypeStruct(tiled, BF16),
         scratch_shapes=[
@@ -352,9 +430,10 @@
             pltpu.VMEM((n, heads, tile_rows * row_count, cols), F32),
             pltpu.VMEM((heads, length, 2 * inner), BF16),
             pltpu.VMEM((2 * inner, length), BF16),
-            pltpu.VMEM((heads * length, inner), BF16),
-            pltpu.VMEM((heads, block, length), F32),
-            pltpu.VMEM((block, heads * length), BF16),
+            pltpu.VMEM((heads, length, inner), BF16),
+            pltpu.VMEM((2, block, length), F32),
+            pltpu.VMEM((2, block, length), BF16),
+            pltpu.VMEM((planes, block, inner), F32),
             pltpu.VMEM((rows, n, cols, channels), BF16),
             dma((rows // chunk,)),
             dma((n, rows // chunk)),
@@ -375,8 +454,8 @@
         ),
         name="gated_attention",
     )(
-        pair.reshape(tiled), norm_gain[None], norm_shift[None], wbt, w_query, w_key.T, w_value,
-        w_gate, gate_shift[None],
+        pair.reshape(tiled), norm_gain[None], norm_shift[None], wbt,
+        jnp.concatenate([w_query, w_value], axis=1), w_key.T, w_gate, gate_shift[None],
     )
 
 

time: 479 us -> 418 us (0.87)
  Pallas kernels: 475 us -> 414 us
    pallas_call x1, Pallas kernels: 464 us -> 403 us  [gated_attention(): pl.pallas_call(functools.partial(fused_body, chunk=chunk), in_specs=[anyw...]
where the time goes in v2:
time: 418 us
  Pallas kernels  414 us (99%)
    pallas_call x1, Pallas kernels, gated_attention(): pl.pallas_call(functools.partial(fused_body, chunk=chunk), in_specs=[anyw...  403 us
    pallas_call x1, Pallas kernels, project_out(): pl.pallas_call(out_body, grid=(tile_rows // step,), in_specs=[pl.BlockSpe...  10.3 us

profile of v2, /device:TPU:0, one launch (start us, length us, event | category | flops | bytes accessed | tf_op | source)
XLA Modules:
  0.0 417.9 jit_solution(17634508863817828551)
XLA Ops:
  0.0 1.3 pad.4.wbt_ref
  1.3 1.5 copy.12
  2.7 1.4 pad_maximum_fusion.wqv_ref
  4.1 403.4 %gated_attention.1 = bf16[8,32,128,128]{3,2,1,0:T(8,128)(2,1)} custom-call(bf16[8,32,128,128]{3,2,1,0:T(8,128)(2,1)} %bitcast.9, f32[1,128]{1,0:T(1,128)} %bitcast.12, f32[1,128]{1,0:T(1,128)} %bitcast.13, f32[16,128]{1,0:T(8,128)} %pad.4.wbt_ref, bf16[128,256]{1,0:T(8,128)(2,1)} %pad_maximum_fusion.wqv_ref, bf16[128,128]{1,0:T(8,128)(2,1)} %bitcast.10, ...), custom_call_target="tpu_custom_call" | custom-call | tf_op jit(solution)/shard_map/gated_attention/pallas_call | solution.py:422
  407.5 10.3 %project_out.1 = bf16[256,128,128]{2,1,0:T(8,128)(2,1)} custom-call(bf16[256,128,128]{2,1,0:T(8,128)(2,1)} %bitcast.8, bf16[128,128]{1,0:T(8,128)(2,1)} %wo_ref.1, f32[1,128]{1,0:T(1,128)} %bitcast.15), custom_call_target="tpu_custom_call" | custom-call | tf_op jit(solution)/shard_map/project_out/pallas_call | solution.py:473

commit v3 on v2

--- a/solution.py
+++ b/solution.py
@@ -114,9 +114,9 @@
 
 
 def fused_body(
-    pair_ref, gain_ref, shift_ref, wbt_ref, wqv_ref, wkt_ref, wg_ref, gshift_ref,
+    pair_ref, gain_ref, shift_ref, wbt_ref, wq_ref, wk_ref, wv_ref, wg_ref, gshift_ref,
     gated_ref,
-    xs_ref, xr_ref, bias_ref, q_ref, kt_ref, v_ref, s_ref, w_ref, sum_ref, g_ref,
+    wqv_ref, wkt_ref, xs_ref, xr_ref, bias_ref, q_ref, kt_ref, v_ref, s_ref, w_ref, sum_ref, g_ref,
     load_sem, x_send, x_recv, own_sem, b_recv, up_send, down_send, side_send, y_send, core_send,
     g_send, g_recv, g_own, *, chunk,
 ):
@@ -226,6 +226,10 @@
 
     norm_chunk(0)
     send_x(0)
+    inner = wq_ref.shape[1]
+    wqv_ref[:, :inner] = wq_ref[...]
+    wqv_ref[:, inner:] = wv_ref[...]
+    wkt_ref[...] = wk_ref[...].T
     for k in range(1, chunks):
         norm_chunk(k)
 
@@ -411,7 +415,6 @@
     length = n * cols
     heads, inner = w_bias.shape[1], w_query.shape[1]
     chunk = math.gcd(rows, 4)
-    wbt = jnp.pad(w_bias.T, ((0, -heads % 16), (0, 0)))
     tiled = (n, rows, cols, channels)
     planes = row_count // (2 if row_count % 2 == 0 else 1)
     block = length // planes
@@ -421,10 +424,12 @@
     anywhere = pl.BlockSpec(memory_space=pl.ANY)
     return pl.pallas_call(
         functools.partial(fused_body, chunk=chunk),
-        in_specs=[anywhere] + [vmem] * 7,
+        in_specs=[anywhere] + [vmem] * 8,
         out_specs=anywhere,
         out_shape=jax.ShapeDtypeStruct(tiled, BF16),
         scratch_shapes=[
+            pltpu.VMEM((channels, 2 * inner), BF16),
+            pltpu.VMEM((inner, channels), BF16),
             pltpu.VMEM(tiled, BF16),
             pltpu.VMEM((rows, n, cols, channels), BF16),
             pltpu.VMEM((n, heads, tile_rows * row_count, cols), F32),
@@ -454,8 +459,8 @@
         ),
         name="gated_attention",
     )(
-        pair.reshape(tiled), norm_gain[None], norm_shift[None], wbt,
-        jnp.concatenate([w_query, w_value], axis=1), w_key.T, w_gate, gate_shift[None],
+        pair.reshape(tiled), norm_gain[None], norm_shift[None], w_bias.T, w_query,
+        w_key, w_value, w_gate, gate_shift[None],
     )
 
 
@@ -469,7 +474,7 @@
 def project_out(gated, w_out, out_shift):
     tile_rows, cols, inner = gated.shape
     channels = w_out.shape[1]
-    step = math.gcd(tile_rows, 32)
+    step = math.gcd(tile_rows, 64)
     return pl.pallas_call(
         out_body,
         grid=(tile_rows // step,),
@@ -480,6 +485,7 @@
         ],
         out_specs=pl.BlockSpec((step, cols, channels), lambda i: (i, 0, 0)),
         out_shape=jax.ShapeDtypeStruct((tile_rows, cols, channels), BF16),
+        compiler_params=pltpu.CompilerParams(vmem_limit_bytes=VMEM_LIMIT),
         name="project_out",
     )(gated, w_out, out_shift[None])
 

time: 418 us -> 412 us (0.986)
  no operation moved by 1% of the time
where the time goes in v3:
time: 412 us
  Pallas kernels  412 us (100%)
    pallas_call x1, Pallas kernels, gated_attention(): pl.pallas_call(functools.partial(fused_body, chunk=chunk), in_specs=[anyw...  403 us

profile of v3, /device:TPU:0, one launch (start us, length us, event | category | flops | bytes accessed | tf_op | source)
XLA Modules:
  0.0 411.6 jit_solution(10296873190850834527)
XLA Ops:
  0.0 403.5 %gated_attention.1 = bf16[8,32,128,128]{3,2,1,0:T(8,128)(2,1)} custom-call(bf16[8,32,128,128]{3,2,1,0:T(8,128)(2,1)} %bitcast.8, f32[1,128]{1,0:T(1,128)} %bitcast.11, f32[1,128]{1,0:T(1,128)} %bitcast.12, f32[4,128]{1,0:T(4,128)} %bitcast.9, bf16[128,128]{1,0:T(8,128)(2,1)} %wq_ref.1, bf16[128,128]{1,0:T(8,128)(2,1)} %wk_ref.1, bf16[128,128]{1,0:T(8,128)(2,1)} %wv_ref.1, ...), custom_call_target="tpu_custom_call" | custom-call | tf_op jit(solution)/shard_map/gated_attention/pallas_call | solution.py:425
  403.5 8.1 %project_out.1 = bf16[256,128,128]{2,1,0:T(8,128)(2,1)} custom-call(bf16[256,128,128]{2,1,0:T(8,128)(2,1)} %bitcast.7, bf16[128,128]{1,0:T(8,128)(2,1)} %wo_ref.1, f32[1,128]{1,0:T(1,128)} %bitcast.10), custom_call_target="tpu_custom_call" | custom-call | tf_op jit(solution)/shard_map/project_out/pallas_call | solution.py:478
